TPU v7x, 512 devices: a whole 4x4x16 slice. The times are simulated.
512 devices in a mesh: seq: 64 (over y, z), req: 8 (over x, core).
Axes of the slice: x: 4, y: 4, z: 16, core: 2. Of those that a mesh axis runs over, the one named last changes fastest.
Arguments:
- new_token_queries: bfloat16 [4, 64, 2048], P(None, 'req'), may hold values from -48 to 48
- new_token_keys: bfloat16 [4, 64, 1024], P(None, 'req'), may hold values from -48 to 48
- new_token_values: bfloat16 [4, 64, 1024], P(None, 'req'), may hold values from -6 to 6
- key_cache: bfloat16 [64, 2048, 1024], P('req', 'seq'), may hold values from -48 to 48
- value_cache: bfloat16 [64, 2048, 1024], P('req', 'seq'), may hold values from -6 to 6
- cache_len: int32 [64], P('req'), may hold values from 1 to 2048, 34816 in all
- resid: bfloat16 [4, 64, 2048], P(None, 'req'), may hold values from -6 to 6
- gain: bfloat16 [2048], replicated, may hold values from 0.5 to 1.5
- w_gate: bfloat16 [2048, 6144], P('seq', 'req'), may hold values from -0.125 to 0.125
- w_up: bfloat16 [2048, 6144], P('seq', 'req'), may hold values from -0.125 to 0.125
- w_down: bfloat16 [6144, 2048], P('req', 'seq'), may hold values from -0.078125 to 0.078125
Outputs:
- out: bfloat16 [4, 64, 2048], P(None, 'req')
All inputs are finite; a program needn't handle non-finite values. No bound on the sum of `cache_len` on one device may be relied on, other than what follows from the above.
Results may differ from a plain program's by a relative error of at most 0.006.
Values may be sent and summed in bfloat16 or wider, within the bound.
A program may use at most 128 MiB of HBM per device.

v0:
```python
import math
import jax
import jax.numpy as jnp
from jax import lax
from jax.sharding import PartitionSpec as P

QUERY_HEADS = 16
KEY_VALUE_HEADS = 8
HEAD_SIZE = 128
DECODE_STEPS = 4
NEG_FILL = -1e30
EPSILON = 1e-06


def page_partial(query_vector, key_row_set, value_row_set, valid):
    scores = jnp.einsum(
        "rkgd,rbkd->rkgb", query_vector, key_row_set, preferred_element_type=jnp.float32
    ) / math.sqrt(HEAD_SIZE)
    inside = valid[:, None, None, :]
    scores = jnp.where(inside, scores, NEG_FILL)
    highest = jnp.max(scores, axis=-1)
    weights = jnp.where(inside, jnp.exp(scores - highest[..., None]), 0.0).astype(jnp.bfloat16)
    totals = jnp.sum(weights.astype(jnp.float32), axis=-1)
    weighted = jnp.einsum(
        "rkgb,rbkd->rkgd", weights, value_row_set, preferred_element_type=jnp.float32
    )
    return (highest, totals, weighted)


def merge_pair(former, latter):
    highest = jnp.maximum(former[0], latter[0])
    first_scale = jnp.exp(former[0] - highest)
    second_scale = jnp.exp(latter[0] - highest)
    totals = first_scale * former[1] + second_scale * latter[1]
    weighted = first_scale[..., None] * former[2] + second_scale[..., None] * latter[2]
    return (highest, totals, weighted)


def body(
    new_token_queries,
    new_token_keys,
    new_token_values,
    key_cache,
    value_cache,
    cache_len,
    resid,
    gain,
    w_gate,
    w_up,
    w_down,
):
    count_of_rows = new_token_queries.shape[1]
    page_length = key_cache.shape[1]
    head_cluster = QUERY_HEADS // KEY_VALUE_HEADS
    slice_width = w_gate.shape[0]
    unit_count = w_gate.shape[1]
    seq_index = lax.axis_index("seq")
    positions = seq_index * page_length + jnp.arange(page_length, dtype=jnp.int32)
    valid = positions[None, :] < cache_len[:, None]
    key_row_set = key_cache.reshape(count_of_rows, page_length, KEY_VALUE_HEADS, HEAD_SIZE)
    value_row_set = value_cache.reshape(count_of_rows, page_length, KEY_VALUE_HEADS, HEAD_SIZE)
    joined = jnp.concatenate([w_gate, w_up], axis=1)
    gain_scale = gain.astype(jnp.float32)
    results = []
    for decode_step_index in range(DECODE_STEPS):
        query_vector = new_token_queries[decode_step_index].reshape(
            count_of_rows, KEY_VALUE_HEADS, head_cluster, HEAD_SIZE
        )
        local = page_partial(query_vector, key_row_set, value_row_set, valid)
        highest = lax.pmax(local[0], "seq")
        factor = jnp.exp(local[0] - highest)
        totals, weighted = lax.psum((factor * local[1], factor[..., None] * local[2]), "seq")
        incoming_keys = jnp.swapaxes(new_token_keys[: decode_step_index + 1], 0, 1).reshape(
            count_of_rows, decode_step_index + 1, KEY_VALUE_HEADS, HEAD_SIZE
        )
        incoming_values = jnp.swapaxes(new_token_values[: decode_step_index + 1], 0, 1).reshape(
            count_of_rows, decode_step_index + 1, KEY_VALUE_HEADS, HEAD_SIZE
        )
        fresh_valid = jnp.ones((count_of_rows, decode_step_index + 1), jnp.bool_)
        fresh = page_partial(query_vector, incoming_keys, incoming_values, fresh_valid)
        combined = merge_pair((highest, totals, weighted), fresh)
        attention = (
            (combined[2] / combined[1][..., None])
            .reshape(count_of_rows, QUERY_HEADS * HEAD_SIZE)
            .astype(jnp.bfloat16)
        )
        attention = lax.optimization_barrier(attention).astype(jnp.float32)
        stream = (resid[decode_step_index].astype(jnp.float32) + attention).astype(jnp.bfloat16)
        stream = lax.optimization_barrier(stream).astype(jnp.float32)
        scaled = lax.rsqrt(jnp.mean(stream * stream, axis=-1, keepdims=True) + EPSILON)
        normed = (stream * scaled * gain_scale).astype(jnp.bfloat16)
        own_slice = lax.dynamic_slice_in_dim(normed, seq_index * slice_width, slice_width, 1)
        partial_sums = jnp.dot(
            lax.all_gather(own_slice, "req", axis=0, tiled=True),
            joined,
            preferred_element_type=jnp.float32,
        )
        whole_sums = lax.psum(partial_sums, "seq")
        hidden = (jax.nn.silu(whole_sums[:, :unit_count]) * whole_sums[:, unit_count:]).astype(
            jnp.bfloat16
        )
        down_sum = lax.psum_scatter(
            jnp.dot(hidden, w_down, preferred_element_type=jnp.float32),
            "req",
            scatter_dimension=0,
            tiled=True,
        )
        stream_slice = lax.dynamic_slice_in_dim(stream, seq_index * slice_width, slice_width, 1)
        out_piece = (stream_slice + down_sum).astype(jnp.bfloat16)
        results.append(lax.all_gather(out_piece, "seq", axis=1, tiled=True))
    return jnp.stack(results)


def solution(mesh):
    placed = (
        P(None, "req", None),
        P(None, "req", None),
        P(None, "req", None),
        P("req", "seq", None),
        P("req", "seq", None),
        P("req"),
        P(None, "req", None),
        P(),
        P("seq", "req"),
        P("seq", "req"),
        P("req", "seq"),
    )
    return jax.shard_map(
        body, mesh=mesh, in_specs=placed, out_specs=P(None, "req", None), check_vma=False
    )
```

profile of v0, /device:TPU:8, one launch (start us, length us, event | category | flops | bytes accessed | tf_op | source)
XLA Modules:
  0.0 1327.7 jit_solution(7573360003918362906)
XLA Ops:
  6.5 0.9 fusion.88
  8.2 1.5 fusion.89
  11.1 261.7 %all-reduce.7 = (f32[8,8,2]{2,1,0:T(8,128)S(1)}, f32[8,8,2]{2,1,0:T(8,128)S(1)}, f32[8,8,2]{2,1,0:T(8,128)S(1)}, f32[8,8,2]{2,1,0:T(8,128)S(1)}) all-reduce(f32[8,8,2]{2,1,0:T(8,128)S(1)} %get-tuple-element.80, f32[8,8,2]{2,1,0:T(8,128)S(1)} %get-tuple-element.78, ...), channel_id=1, replica_groups=mesh['seq'=64,'req'=8] {'seq'}, use_global_device_ids=true, to_apply=%region_29.30 | all-reduce | flops 512 | bytes 4096 | tf_op jit(solution)/shard_map/pmax | solution.py:70
  273.5 0.9 convolution_multiply_fusion.11
  274.4 0.9 convolution_multiply_fusion.9
  276.2 0.9 convolution_multiply_fusion.5
  280.1 274.1 %all-reduce.4 = (f32[8,8,2]{2,1,0:T(8,128)S(1)}, f32[8,8,2]{2,1,0:T(8,128)S(1)}, f32[8,8,2]{2,1,0:T(8,128)S(1)}, f32[8,8,2]{2,1,0:T(8,128)S(1)}) all-reduce(f32[8,8,2]{2,1,0:T(8,128)S(1)} %get-tuple-element.88, f32[8,8,2]{2,1,0:T(8,128)S(1)} %get-tuple-element.47, ...), channel_id=1, replica_groups=mesh['seq'=64,'req'=8] {'seq'}, use_global_device_ids=true, to_apply=%region_33.34 | all-reduce | flops 512 | bytes 4096 | tf_op jit(solution)/shard_map/psum | solution.py:72
  556.6 1.2 fusion.11
  562.6 12.0 all_gather.24
  574.6 11.2 all_gather.26
  585.8 0.9 fusion.95
  586.8 0.9 fusion.96
  587.7 11.3 all_gather.28
  599.0 0.9 fusion.97
  599.9 11.2 all_gather.30
  611.2 0.9 fusion.98
  612.1 1.3 dynamic-slice
  614.0 286.2 %all-reduce.12.cloned.1.call-done = (f32[64,1536]{1,0:T(8,128)}, f32[64,1536]{1,0:T(8,128)}, f32[64,1536]{1,0:T(8,128)}, f32[64,1536]{1,0:T(8,128)}) async-done(((f32[64,1536]{1,0:T(8,128)}, f32[64,1536]{1,0:T(8,128)}, f32[64,1536]{1,0:T(8,128)}, f32[64,1536]{1,0:T(8,128)}), (f32[64,1536]{1,0:T(8,128)}, f32[64,1536]{1,0:T(8,128)}, f32[64,1536]{1,0:T(8,128)}, ...) | async-done | bytes 1572880 | tf_op jit(solution)/shard_map/psum | solution.py:98
  900.2 1.2 fusion.33
  903.7 24.8 %all-reduce.8 = (f32[64,32]{1,0:T(8,128)S(1)}, f32[64,32]{1,0:T(8,128)S(1)}, f32[64,32]{1,0:T(8,128)S(1)}, f32[64,32]{1,0:T(8,128)S(1)}) all-reduce(f32[64,32]{1,0:T(8,128)S(1)} %fusion.39, f32[64,32]{1,0:T(8,128)S(1)} %fusion.37, f32[64,32]{1,0:T(8,128)S(1)} %fusion.35, ...), channel_id=5, replica_groups=mesh['seq'=64,'req'=8] {'req'}, use_global_device_ids=true, to_apply=%region_37.38.clone | all-reduce | flops 8192 | bytes 65536
  928.6 97.9 %all-gather = bf16[64,32,8]{1,2,0:T(8,128)(2,1)S(1)} all-gather(bf16[1,32,8]{1,2,0:T(8,128)(2,1)S(1)} %fusion.68), channel_id=1, replica_groups=mesh['seq'=64,'req'=8] {'seq'}, dimensions={0}, use_global_device_ids=true | all-gather | bytes 33280 | tf_op jit(solution)/shard_map/all_gather | solution.py:110
  1026.8 97.5 %all-gather.1 = bf16[64,32,8]{1,2,0:T(8,128)(2,1)S(1)} all-gather(bf16[1,32,8]{1,2,0:T(8,128)(2,1)S(1)} %fusion.69), channel_id=1, replica_groups=mesh['seq'=64,'req'=8] {'seq'}, dimensions={0}, use_global_device_ids=true | all-gather | bytes 33280 | tf_op jit(solution)/shard_map/all_gather | solution.py:110
  1124.5 97.6 %all-gather.2 = bf16[64,32,8]{1,2,0:T(8,128)(2,1)S(1)} all-gather(bf16[1,32,8]{1,2,0:T(8,128)(2,1)S(1)} %fusion.70), channel_id=1, replica_groups=mesh['seq'=64,'req'=8] {'seq'}, dimensions={0}, use_global_device_ids=true | all-gather | bytes 33280 | tf_op jit(solution)/shard_map/all_gather | solution.py:110
  1222.5 97.5 %all-gather.3 = bf16[64,32,8]{1,2,0:T(8,128)(2,1)S(1)} all-gather(bf16[1,32,8]{1,2,0:T(8,128)(2,1)S(1)} %fusion.71), channel_id=1, replica_groups=mesh['seq'=64,'req'=8] {'seq'}, dimensions={0}, use_global_device_ids=true | all-gather | bytes 33280 | tf_op jit(solution)/shard_map/all_gather | solution.py:110
  (115 shorter events, 17.7 us)
Async XLA Ops:
  6.5 267.0 %copy-start = (bf16[8,32,1024]{2,1,0:T(8,128)(2,1)S(1)}, bf16[8,32,1024]{2,1,0:T(8,128)(2,1)}, u32[]{:S(2)}) copy-start(bf16[8,32,1024]{2,1,0:T(8,128)(2,1)} %param.15) | copy-start | bytes 1572868
  6.5 550.0 %all-reduce.14.cloned.1.call-start = ((), (), s32[]{:S(2)}) async-start(), calls=%async_computation.1 | async-start | bytes 524288 | tf_op jit(solution)/shard_map/psum | solution.py:72
  7.4 0.7 copy-start.7
  7.5 2.2 copy-start.8
  277.0 0.8 copy-start.1
  277.1 0.9 copy-start.2
  277.1 623.2 %all-reduce.12.cloned.1.call-start = ((), (), s32[]{:S(2)}) async-start(), calls=%async_computation | async-start | bytes 3145728 | tf_op jit(solution)/shard_map/psum | solution.py:98
  279.0 0.8 copy-start.5
  554.5 0.8 copy-start.6
  557.8 0.8 copy-start.13
  559.0 0.8 copy-start.12
  560.1 0.8 copy-start.4
  561.0 0.9 copy-start.3
  612.1 288.2 %copy-start.14 = (bf16[768,32]{0,1:T(8,128)(2,1)S(1)}, bf16[768,32]{0,1:T(8,128)(2,1)}, u32[]{:S(2)}) copy-start(bf16[768,32]{0,1:T(8,128)(2,1)} %param.21) | copy-start | bytes 147460
  900.2 1.3 copy-start.11
  901.5 1.0 copy-start.10
  902.5 1.0 copy-start.9
Sparse Core Ops, SparseCore 0:
  277.2 274.5 all-reduce.13
  612.2 287.9 all-reduce.11
where the time goes:
time: 1330 us
  blocking collectives  997 us (75%)
  waiting for transfers between devices  286 us (22%)
  matrix products  14.7 us (1%)
  between operations  14.5 us (1%)
    all_gather x4, blocking collectives, body(): results.append(lax.all_gather(out_piece, 'seq', axis=1, tiled=True))  391 us
    psum x1, waiting for transfers between devices, body(): whole_sums = lax.psum(partial_sums, 'seq')  286 us
    psum x1, blocking collectives, body(): lax.psum((factor * local[1], factor[..., None] * local[2]), 'seq')  274 us
    pmax x1, blocking collectives, body(): highest = lax.pmax(local[0], 'seq')  262 us
    all_gather x4, blocking collectives, body(): lax.all_gather(own_slice, 'req', axis=0, tiled=True)  45.8 us
  transfers between devices with their start and end apart: 2, of which 1 were waited for; matrix products, arithmetic and copies ran while one was open for 0% of the time, Pallas kernels for 0%

commit v1 on v0

--- a/solution.py
+++ b/solution.py
@@ -95,7 +95,8 @@
             joined,
             preferred_element_type=jnp.float32,
         )
-        whole_sums = lax.psum(partial_sums, "seq")
+        parts = lax.all_gather(partial_sums, "seq")
+        whole_sums = jnp.sum(parts, axis=0)
         hidden = (jax.nn.silu(whole_sums[:, :unit_count]) * whole_sums[:, unit_count:]).astype(
             jnp.bfloat16
         )

time: 1330 us -> 2010 us (1.51)
  the two profiles are of different devices: /device:TPU:8 before, /device:TPU:32 now
where the time goes in v1:
time: 2010 us
  blocking collectives  1020 us (51%)
  waiting for transfers between devices  897 us (45%)
  other arithmetic  44.2 us (2%)
    all_gather x4, waiting for transfers between devices, body(): parts = lax.all_gather(partial_sums, 'seq')  897 us
    all_gather x4, blocking collectives, body(): results.append(lax.all_gather(out_piece, 'seq', axis=1, tiled=True))  392 us
    pmax x1, blocking collectives, body(): highest = lax.pmax(local[0], 'seq')  280 us
    psum x1, blocking collectives, body(): lax.psum((factor * local[1], factor[..., None] * local[2]), 'seq')  276 us
    all_gather x4, blocking collectives, body(): lax.all_gather(own_slice, 'req', axis=0, tiled=True)  45.7 us
  transfers between devices with their start and end apart: 5, of which 4 were waited for; matrix products, arithmetic and copies ran while one was open for 2% of the time, Pallas kernels for 0%

profile of v1, /device:TPU:32, one launch (start us, length us, event | category | flops | bytes accessed | tf_op | source)
XLA Modules:
  0.0 2006.5 jit_solution(17208133815654008652)
XLA Ops:
  8.2 1.5 fusion.89
  9.7 1.5 fusion.90
  11.2 1.5 fusion.91
  12.8 1.5 fusion.92
  14.3 280.4 %all-reduce.6 = (f32[8,8,2]{2,1,0:T(8,128)S(1)}, f32[8,8,2]{2,1,0:T(8,128)S(1)}, f32[8,8,2]{2,1,0:T(8,128)S(1)}, f32[8,8,2]{2,1,0:T(8,128)S(1)}) all-reduce(f32[8,8,2]{2,1,0:T(8,128)S(1)} %get-tuple-element.76, f32[8,8,2]{2,1,0:T(8,128)S(1)} %get-tuple-element.74, ...), channel_id=1, replica_groups=mesh['seq'=64,'req'=8] {'seq'}, use_global_device_ids=true, to_apply=%region_29.30 | all-reduce | flops 512 | bytes 4096 | tf_op jit(solution)/shard_map/pmax | solution.py:70
  306.7 276.4 %all-reduce.4 = (f32[8,8,2]{2,1,0:T(8,128)S(1)}, f32[8,8,2]{2,1,0:T(8,128)S(1)}, f32[8,8,2]{2,1,0:T(8,128)S(1)}, f32[8,8,2]{2,1,0:T(8,128)S(1)}) all-reduce(f32[8,8,2]{2,1,0:T(8,128)S(1)} %get-tuple-element.84, f32[8,8,2]{2,1,0:T(8,128)S(1)} %get-tuple-element.43, ...), channel_id=1, replica_groups=mesh['seq'=64,'req'=8] {'seq'}, use_global_device_ids=true, to_apply=%region_33.34 | all-reduce | flops 512 | bytes 4096 | tf_op jit(solution)/shard_map/psum | solution.py:72
  592.0 11.9 all_gather.48
  604.9 11.2 all_gather.52
  617.2 11.3 all_gather.56
  629.5 11.2 all_gather.60
  641.7 1.3 dynamic-slice
  643.6 193.7 %all-gather.13.cloned.1.call-done = f32[4096,1536]{1,0:T(8,128)} async-done(((f32[64,1536]{1,0:T(8,128)}), f32[4096,1536]{1,0:T(8,128)}) %all-gather.13.cloned.1.call-update) | async-done | bytes 25165840 | tf_op jit(solution)/shard_map/all_gather | solution.py:98
  837.3 9.4 reduce_sum.141
  846.8 234.8 %all-gather.15.cloned.1.call-done = f32[4096,1536]{1,0:T(8,128)} async-done(((f32[64,1536]{1,0:T(8,128)}), f32[4096,1536]{1,0:T(8,128)}) %all-gather.15.cloned.1.call-update) | async-done | bytes 25165840 | tf_op jit(solution)/shard_map/all_gather | solution.py:98
  1081.6 9.4 reduce_sum.145
  1091.0 234.6 %all-gather.17.cloned.1.call-done = f32[4096,1536]{1,0:T(8,128)} async-done(((f32[64,1536]{1,0:T(8,128)}), f32[4096,1536]{1,0:T(8,128)}) %all-gather.17.cloned.1.call-update) | async-done | bytes 25165840 | tf_op jit(solution)/shard_map/all_gather | solution.py:98
  1325.6 9.5 reduce_sum.149
  1335.7 234.0 %all-gather.19.cloned.1.call-done = f32[4096,1536]{1,0:T(8,128)} async-done(((f32[64,1536]{1,0:T(8,128)}), f32[4096,1536]{1,0:T(8,128)}) %all-gather.19.cloned.1.call-update) | async-done | bytes 25165840 | tf_op jit(solution)/shard_map/all_gather | solution.py:98
  1569.7 9.4 reduce_sum.153
  1579.3 26.5 %all-reduce.7 = (f32[64,32]{1,0:T(8,128)S(1)}, f32[64,32]{1,0:T(8,128)S(1)}, f32[64,32]{1,0:T(8,128)S(1)}, f32[64,32]{1,0:T(8,128)S(1)}) all-reduce(f32[64,32]{1,0:T(8,128)S(1)} %fusion.39, f32[64,32]{1,0:T(8,128)S(1)} %fusion.37, f32[64,32]{1,0:T(8,128)S(1)} %fusion.35, ...), channel_id=9, replica_groups=mesh['seq'=64,'req'=8] {'req'}, use_global_device_ids=true, to_apply=%region_37.38.clone | all-reduce | flops 8192 | bytes 65536
  1605.9 99.1 %all-gather.4 = bf16[64,32,8]{1,2,0:T(8,128)(2,1)S(1)} all-gather(bf16[1,32,8]{1,2,0:T(8,128)(2,1)S(1)} %fusion.68), channel_id=1, replica_groups=mesh['seq'=64,'req'=8] {'seq'}, dimensions={0}, use_global_device_ids=true | all-gather | bytes 33280 | tf_op jit(solution)/shard_map/all_gather | solution.py:111
  1705.3 98.1 %all-gather.5 = bf16[64,32,8]{1,2,0:T(8,128)(2,1)S(1)} all-gather(bf16[1,32,8]{1,2,0:T(8,128)(2,1)S(1)} %fusion.69), channel_id=1, replica_groups=mesh['seq'=64,'req'=8] {'seq'}, dimensions={0}, use_global_device_ids=true | all-gather | bytes 33280 | tf_op jit(solution)/shard_map/all_gather | solution.py:111
  1803.7 97.1 %all-gather.6 = bf16[64,32,8]{1,2,0:T(8,128)(2,1)S(1)} all-gather(bf16[1,32,8]{1,2,0:T(8,128)(2,1)S(1)} %fusion.70), channel_id=1, replica_groups=mesh['seq'=64,'req'=8] {'seq'}, dimensions={0}, use_global_device_ids=true | all-gather | bytes 33280 | tf_op jit(solution)/shard_map/all_gather | solution.py:111
  1901.0 98.1 %all-gather.7 = bf16[64,32,8]{1,2,0:T(8,128)(2,1)S(1)} all-gather(bf16[1,32,8]{1,2,0:T(8,128)(2,1)S(1)} %fusion.71), channel_id=1, replica_groups=mesh['seq'=64,'req'=8] {'seq'}, dimensions={0}, use_global_device_ids=true | all-gather | bytes 33280 | tf_op jit(solution)/shard_map/all_gather | solution.py:111
  (104 shorter events, 28.8 us)
Async XLA Ops:
  6.5 288.9 %copy-start = (bf16[8,32,1024]{2,1,0:T(8,128)(2,1)S(1)}, bf16[8,32,1024]{2,1,0:T(8,128)(2,1)}, u32[]{:S(2)}) copy-start(bf16[8,32,1024]{2,1,0:T(8,128)(2,1)} %param.15) | copy-start | bytes 1572868
  6.5 579.0 %all-reduce.10.cloned.1.call-start = ((), (), s32[]{:S(2)}) async-start(), calls=%async_computation.4 | async-start | bytes 524288 | tf_op jit(solution)/shard_map/psum | solution.py:72
  299.0 538.4 %all-gather.13.cloned.1.call-start = ((), (), s32[]{:S(2)}) async-start(), calls=%async_computation | async-start | bytes 25559040 | tf_op jit(solution)/shard_map/all_gather | solution.py:98
  604.8 476.7 %all-gather.15.cloned.1.call-start = ((), (), s32[]{:S(2)}) async-start(), calls=%async_computation.1 | async-start | bytes 25559040 | tf_op jit(solution)/shard_map/all_gather | solution.py:98
  617.1 708.5 %all-gather.17.cloned.1.call-start = ((), (), s32[]{:S(2)}) async-start(), calls=%async_computation.2 | async-start | bytes 25559040 | tf_op jit(solution)/shard_map/all_gather | solution.py:98
  629.4 940.3 %all-gather.19.cloned.1.call-start = ((), (), s32[]{:S(2)}) async-start(), calls=%async_computation.3 | async-start | bytes 25559040 | tf_op jit(solution)/shard_map/all_gather | solution.py:98
  1081.6 253.5 %copy-start.2 = (bf16[768,32]{0,1:T(8,128)(2,1)S(1)}, bf16[768,32]{0,1:T(8,128)(2,1)}, u32[]{:S(2)}) copy-start(bf16[768,32]{0,1:T(8,128)(2,1)} %param.21) | copy-start | bytes 147460
  1325.6 674.3 %copy-start.1 = (bf16[8,32,1024]{2,1,0:T(8,128)(2,1)S(1)}, bf16[8,32,1024]{2,1,0:T(8,128)(2,1)}, u32[]{:S(2)}) copy-start(bf16[8,32,1024]{2,1,0:T(8,128)(2,1)} %param.15) | copy-start | bytes 1572868
Sparse Core Ops, SparseCore 0:
  299.1 255.9 all-reduce.9
  605.0 232.3 all-gather.12
  840.7 240.7 all-gather.14
  1084.8 240.7 all-gather.16
  1328.8 240.7 all-gather.18
